TPU v7x, 768 devices: a whole 4x8x12 slice. The times are simulated.
768 devices in a mesh: gx: 64 (over y, z_hi, core), gy: 12 (over z_lo, x).
Axes of the slice: x: 4, y: 8, z: 12 (z_hi: 4, z_lo: 3; z = z_hi * 3 + z_lo), core: 2. Of those that a mesh axis runs over, the one named last changes fastest.
Arguments:
- state: float32 [9, 56, 98304], P(None, None, ('gx', 'gy')), may hold values from -6 to 6
- star_matrices: float32 [3, 9, 9, 98304], P(None, None, None, ('gx', 'gy')), may hold values from -1.25 to 1.25
- stiffness: float32 [3, 56, 56], replicated, may hold values from -0.75 to 0.75
- face_project: float32 [4, 21, 56], replicated, may hold values from -0.75 to 0.75
- flux_inner: float32 [9, 9], replicated, may hold values from -2 to 2
- flux_outer: float32 [9, 9], replicated, may hold values from -2 to 2
- rate_level: int32 [98304], P(('gx', 'gy')), may hold values from 0 to 2
- neighbour: int32 [4, 98304], P(None, ('gx', 'gy')), may hold values from 0 to 511
- send_slots: int32 [4, 196608], P(None, ('gx', 'gy')), may hold values from 0 to 511
- receive_slots: int32 [4, 196608], P(None, ('gx', 'gy')), may hold values from 0 to 511
- fault_faces: int32 [49152], P(('gx', 'gy')), may hold values from 0 to 511, as said below
- slip_flags: int32 [49152], P(('gx', 'gy')), may hold values 0 or 1
Outputs:
- updated: float32 [9, 56, 98304], P(None, None, ('gx', 'gy'))
Inputs may be any that keep to these rules, and one draw needn't show every extreme that they name: `neighbour`: local face indices f * 128 + e of the device's own elements. `send_slots`: local face indices of the sending device's own elements. `receive_slots`: local face indices of the receiving device's own elements; two slots may act on one face. `fault_faces`: local face indices of the device's own elements, distinct within one device.
All inputs are finite; a program needn't handle non-finite values. No bound on the sum of `slip_flags` on one device may be relied on, other than what follows from the above.
Results may differ from a plain program's by a relative error of at most 0.0003.
Values sent between devices are 32-bit elements; how exact they have to be, the bound alone decides.
No kernel may reach another device: no remote copies, remote signals or barrier semaphores. Data moves between devices by JAX's collectives and lax.ppermute only.
A program may use at most 64 MiB of HBM per device.

v0:
```python
import jax
import jax.numpy as jnp
from jax import lax
from jax.sharding import PartitionSpec as P

FIELDS = 9
FACE_MODES = 21
ORDER = 6


coarse_dt = 2.0
slip_keep = 0.3


def shifted(value, axis, steps):
    count = lax.axis_size(axis)
    first, last = (max(0, -steps), min(count, count - steps))
    return lax.ppermute(value, axis, [(source, source + steps) for source in range(first, last)])


def taylor_terms(rate_level):
    step_size = coarse_dt * jnp.exp2(-rate_level.astype(jnp.float32))
    terms = []
    factor = step_size
    for degree in range(ORDER):
        terms.append(factor)
        factor = factor * step_size / (degree + 2.0)
    return terms


def star_apply(star_matrices, modal):
    return jnp.sum(star_matrices[:, :, :, None, :] * modal[:, :, None, :, :], axis=(0, 1))


def derive(current, star_matrices, stiffness):
    modal = jnp.einsum("dmn,qne->dqme", stiffness, current, precision=lax.Precision.HIGHEST)
    return -star_apply(star_matrices, modal)


def volume_term(integral, star_matrices, stiffness):
    modal = jnp.einsum("dnm,qne->dqme", stiffness, integral, precision=lax.Precision.HIGHEST)
    return star_apply(star_matrices, modal)


def on_faces(field, face_project):
    faces = jnp.einsum("fjn,qne->qjfe", face_project, field, precision=lax.Precision.HIGHEST)
    return faces.reshape(FIELDS * FACE_MODES, -1)


def lift_faces(face_terms, face_project):
    shaped = face_terms.reshape(FIELDS, FACE_MODES, 4, -1)
    return jnp.einsum("fjm,qjfe->qme", face_project, shaped, precision=lax.Precision.HIGHEST)


def apply_flux(matrix, face_terms):
    shaped = face_terms.reshape(FIELDS, FACE_MODES, -1)
    mixed = jnp.einsum("qp,qjx->pjx", matrix, shaped, precision=lax.Precision.HIGHEST)
    return mixed.reshape(FIELDS * FACE_MODES, -1)


def keep_mask(fault_faces, slip_flags, count):
    slide = jnp.zeros((4 * count,), jnp.float32).at[fault_faces].set(slip_flags.astype(jnp.float32))
    fields = jnp.arange(FIELDS)
    shear = ((fields >= 3) & (fields < 6)).astype(jnp.float32)
    keep = 1.0 - (1.0 - slip_keep) * shear[:, None] * slide[None, :]
    return jnp.repeat(keep, FACE_MODES, axis=0)


def move_stack(piece, direction):
    if direction < 2:
        return shifted(piece, "gx", 1 - 2 * direction)
    return shifted(piece, "gy", 1 - 2 * (direction - 2))


def weigh_stack(terms, stack):
    arrived = terms[0][None, :] * stack[0]
    for degree in range(1, ORDER):
        arrived = arrived + terms[degree][None, :] * stack[degree]
    return arrived


def shards(
    state,
    star_matrices,
    stiffness,
    face_project,
    flux_inner,
    flux_outer,
    rate_level,
    neighbour,
    send_slots,
    receive_slots,
    fault_faces,
    slip_flags,
):
    count = state.shape[-1]
    terms = taylor_terms(rate_level)
    current = state
    integral = terms[0] * state
    outer = jnp.zeros((FIELDS * FACE_MODES, 4 * count), jnp.float32)
    flat_neighbour = neighbour.reshape(-1)
    sent = []
    for degree in range(ORDER):
        if degree > 0:
            current = derive(current, star_matrices, stiffness)
            integral = integral + terms[degree] * current
        faces = on_faces(current, face_project)
        outer = outer + jnp.tile(terms[degree], 4)[None, :] * faces[:, flat_neighbour]
        sent.append(faces[:, send_slots])
    stacks = jnp.stack(sent)
    target_level = rate_level[receive_slots % count]
    for direction in range(4):
        incoming = move_stack(stacks[:, :, direction, :], direction)
        arrived = weigh_stack([part[direction] for part in taylor_terms(target_level)], incoming)
        outer = outer.at[:, receive_slots[direction]].add(arrived)
    inner = on_faces(integral, face_project)
    keep = keep_mask(fault_faces, slip_flags, count)
    flux = apply_flux(flux_inner, inner) + apply_flux(flux_outer, outer * keep)
    return state + volume_term(integral, star_matrices, stiffness) + lift_faces(flux, face_project)


def solution(mesh):
    placed = (
        P(None, None, ("gx", "gy")),
        P(None, None, None, ("gx", "gy")),
        P(),
        P(),
        P(),
        P(),
        P(("gx", "gy")),
        P(None, ("gx", "gy")),
        P(None, ("gx", "gy")),
        P(None, ("gx", "gy")),
        P(("gx", "gy")),
        P(("gx", "gy")),
    )
    return jax.shard_map(
        shards, mesh=mesh, in_specs=placed, out_specs=P(None, None, ("gx", "gy")), check_vma=False
    )
```

profile of v0, /device:TPU:54, one launch (start us, length us, event | category | flops | bytes accessed | tf_op | source)
XLA Modules:
  0.0 176.3 jit_solution(1758242041419718222)
XLA Ops:
  0.0 1.0 copy.182
  1.0 1.8 %convolution_bitcast_fusion.5 = f32[3,9,56,128]{3,2,0,1:T(8,128)S(1)} fusion(f32[9,56,128]{2,1,0:T(8,128)} %param.12, f32[3,56,56]{2,1,0:T(8,128)S(1)} %copy-done), kind=kOutput, calls=%fused_computation.29 | convolution fusion | flops 130056192 | bytes 1069824 | tf_op jit(solution)/shard_map/dmn,qne->dqme/dot_general | solution.py:36
  3.5 0.8 convolution_bitcast_fusion.4
  5.0 0.8 convolution_bitcast_fusion.3
  6.5 0.8 convolution_bitcast_fusion.2
  8.0 0.8 convolution_bitcast_fusion.1
  13.6 1.2 copy.211
  15.0 0.8 copy.256
  15.8 1.2 copy.208
  17.1 0.8 copy.255
  17.9 1.2 copy.205
  19.3 0.8 copy.254
  20.1 1.2 copy.202
  22.2 1.4 copy.199
  24.5 1.2 copy.196
  25.8 4.7 %gather_fusion.7 = f32[1024,189]{1,0:T(8,128)} fusion(f32[189,512]{0,1:T(8,128)S(1)} %copy.196, s32[1024]{0:T(1024)S(1)} %broadcast_clamp_fusion.1), kind=kCustom, calls=%fused_computation.7 | custom fusion | bytes 1552384 | tf_op jit(solution)/shard_map/gather | solution.py:109
  30.5 2.4 %copy.213 = f32[4,256,189]{1,2,0:T(8,128)} copy(f32[4,256,189]{2,1,0:T(8,128)} %bitcast.440) | data formatting | bytes 1548288 | tf_op jit(solution)/shard_map/gather | solution.py:109
  32.9 2.0 %bitcast_dynamic-update-slice_fusion.5 = f32[6,189,4,256]{3,1,0,2:T(8,128)} fusion(f32[4,256,189]{1,2,0:T(8,128)} %copy.213), kind=kLoop, calls=%fused_computation.50 | loop fusion | bytes 1560576
  35.0 4.7 %gather_fusion.8 = f32[1024,189]{1,0:T(8,128)} fusion(f32[189,512]{0,1:T(8,128)S(1)} %copy.199, s32[1024]{0:T(1024)S(1)} %broadcast_clamp_fusion.1), kind=kCustom, calls=%fused_computation.8 | custom fusion | bytes 1552384 | tf_op jit(solution)/shard_map/gather | solution.py:109
  39.7 2.4 %copy.215 = f32[4,256,189]{1,2,0:T(8,128)} copy(f32[4,256,189]{2,1,0:T(8,128)} %bitcast.441) | data formatting | bytes 1548288 | tf_op jit(solution)/shard_map/gather | solution.py:109
  42.1 4.7 %gather_fusion.9 = f32[1024,189]{1,0:T(8,128)} fusion(f32[189,512]{0,1:T(8,128)S(1)} %copy.202, s32[1024]{0:T(1024)S(1)} %broadcast_clamp_fusion.1), kind=kCustom, calls=%fused_computation.9 | custom fusion | bytes 1552384 | tf_op jit(solution)/shard_map/gather | solution.py:109
  46.9 2.4 %copy.217 = f32[4,256,189]{1,2,0:T(8,128)} copy(f32[4,256,189]{2,1,0:T(8,128)} %bitcast.442) | data formatting | bytes 1548288 | tf_op jit(solution)/shard_map/gather | solution.py:109
  49.3 4.7 %gather_fusion.10 = f32[1024,189]{1,0:T(8,128)} fusion(f32[189,512]{0,1:T(8,128)S(1)} %copy.205, s32[1024]{0:T(1024)S(1)} %broadcast_clamp_fusion.1), kind=kCustom, calls=%fused_computation.10 | custom fusion | bytes 1552384 | tf_op jit(solution)/shard_map/gather | solution.py:109
  54.0 2.4 %copy.219 = f32[4,256,189]{1,2,0:T(8,128)} copy(f32[4,256,189]{2,1,0:T(8,128)} %bitcast.443) | data formatting | bytes 1548288 | tf_op jit(solution)/shard_map/gather | solution.py:109
  56.4 4.7 %gather_fusion.11 = f32[1024,189]{1,0:T(8,128)} fusion(f32[189,512]{0,1:T(8,128)S(1)} %copy.208, s32[1024]{0:T(1024)S(1)} %broadcast_clamp_fusion.1), kind=kCustom, calls=%fused_computation.11 | custom fusion | bytes 1552384 | tf_op jit(solution)/shard_map/gather | solution.py:109
  61.2 2.5 %copy.221 = f32[4,256,189]{1,2,0:T(8,128)} copy(f32[4,256,189]{2,1,0:T(8,128)} %bitcast.444) | data formatting | bytes 1548288 | tf_op jit(solution)/shard_map/gather | solution.py:109
  63.6 4.7 %gather_fusion.12 = f32[1024,189]{1,0:T(8,128)} fusion(f32[189,512]{0,1:T(8,128)S(1)} %copy.211, s32[1024]{0:T(1024)S(1)} %broadcast_clamp_fusion.1), kind=kCustom, calls=%fused_computation.12 | custom fusion | bytes 1552384 | tf_op jit(solution)/shard_map/gather | solution.py:109
  68.4 2.4 %copy.223 = f32[4,256,189]{1,2,0:T(8,128)} copy(f32[4,256,189]{2,1,0:T(8,128)} %bitcast.439) | data formatting | bytes 1548288 | tf_op jit(solution)/shard_map/gather | solution.py:109
  70.8 2.2 %bitcast_dynamic-update-slice_fusion.4 = f32[6,189,4,256]{3,1,0,2:T(8,128)} fusion(f32[6,189,4,256]{3,1,0,2:T(8,128)} %bitcast_dynamic-update-slice_fusion.5, f32[4,256,189]{1,2,0:T(8,128)} %copy.215), kind=kLoop, calls=%fused_computation.49 | loop fusion | bytes 1572864
  73.0 2.1 %bitcast_dynamic-update-slice_fusion.3 = f32[6,189,4,256]{3,1,0,2:T(8,128)} fusion(f32[6,189,4,256]{3,1,0,2:T(8,128)} %bitcast_dynamic-update-slice_fusion.4, f32[4,256,189]{1,2,0:T(8,128)} %copy.217), kind=kLoop, calls=%fused_computation.48 | loop fusion | bytes 1572864
  75.1 2.1 %bitcast_dynamic-update-slice_fusion.2 = f32[6,189,4,256]{3,1,0,2:T(8,128)} fusion(f32[6,189,4,256]{3,1,0,2:T(8,128)} %bitcast_dynamic-update-slice_fusion.3, f32[4,256,189]{1,2,0:T(8,128)} %copy.219), kind=kLoop, calls=%fused_computation.47 | loop fusion | bytes 1572864
  77.1 0.9 bitcast_dynamic-update-slice_fusion.1
  78.1 0.9 bitcast_dynamic-update-slice_fusion
  79.0 4.7 %slice_bitcast_fusion = (f32[6,189,256]{2,1,0:T(8,128)}, f32[6,189,256]{2,1,0:T(8,128)}, f32[6,189,256]{2,1,0:T(8,128)}, f32[6,189,256]{2,1,0:T(8,128)}) fusion(f32[6,189,4,256]{3,1,0,2:T(8,128)} %bitcast_dynamic-update-slice_fusion), kind=kLoop, calls=%fused_computation.39 | loop fusion | bytes 9289728 | tf_op jit(solution)/shard_map/squeeze | solution.py:113
  83.7 1.9 %collective-permute-start = (f32[6,189,256]{2,1,0:T(8,128)}, f32[6,189,256]{2,1,0:T(8,128)}, u32[]{:S(2)}, u32[]{:S(2)}) collective-permute-start(f32[6,189,256]{2,1,0:T(8,128)} %get-tuple-element.10), channel_id=1, source_target_pairs={{0,12},{12,24},{24,36},{36,48},{48,60},{60,72},{72,84},{84,96},{96... | collective-permute-start | bytes 3483656 | tf_op jit(solution)/shard_map/ppermute | solution.py:18
  85.7 14.8 %collective-permute-start.1 = (f32[6,189,256]{2,1,0:T(8,128)}, f32[6,189,256]{2,1,0:T(8,128)}, u32[]{:S(2)}, u32[]{:S(2)}) collective-permute-start(f32[6,189,256]{2,1,0:T(8,128)} %get-tuple-element.9), channel_id=1, source_target_pairs={{12,0},{24,12},{36,24},{48,36},{60,48},{72,60},{84,72},{96,84},{10... | collective-permute-start | bytes 3483656 | tf_op jit(solution)/shard_map/ppermute | solution.py:18
  100.5 3.3 %collective-permute-start.2 = (f32[6,189,256]{2,1,0:T(8,128)}, f32[6,189,256]{2,1,0:T(8,128)}, u32[]{:S(2)}, u32[]{:S(2)}) collective-permute-start(f32[6,189,256]{2,1,0:T(8,128)} %get-tuple-element.8), channel_id=1, source_target_pairs={{0,1},{1,2},{2,3},{3,4},{4,5},{5,6},{6,7},{7,8},{8,9},{9,10},{10,1... | collective-permute-start | bytes 3483656 | tf_op jit(solution)/shard_map/ppermute | solution.py:18
  103.8 2.6 %collective-permute-start.3 = (f32[6,189,256]{2,1,0:T(8,128)}, f32[6,189,256]{2,1,0:T(8,128)}, u32[]{:S(2)}, u32[]{:S(2)}) collective-permute-start(f32[6,189,256]{2,1,0:T(8,128)} %get-tuple-element.7), channel_id=1, source_target_pairs={{1,0},{2,1},{3,2},{4,3},{5,4},{6,5},{7,6},{8,7},{9,8},{10,9},{11,1... | collective-permute-start | bytes 3483656 | tf_op jit(solution)/shard_map/ppermute | solution.py:18
  106.4 2.2 %gather_fusion.5 = f32[512,189]{1,0:T(8,128)} fusion(f32[189,512]{0,1:T(8,128)S(1)} %copy.211, s32[1024]{0:T(1024)S(1)} %get-tuple-element.48), kind=kCustom, calls=%fused_computation.5 | custom fusion | bytes 776192 | tf_op jit(solution)/shard_map/gather | solution.py:108
  108.6 2.2 %gather_fusion.4 = f32[512,189]{1,0:T(8,128)} fusion(f32[189,512]{0,1:T(8,128)S(1)} %copy.208, s32[1024]{0:T(1024)S(1)} %get-tuple-element.48), kind=kCustom, calls=%fused_computation.4 | custom fusion | bytes 776192 | tf_op jit(solution)/shard_map/gather | solution.py:108
  110.9 2.2 %gather_fusion.3 = f32[512,189]{1,0:T(8,128)} fusion(f32[189,512]{0,1:T(8,128)S(1)} %copy.205, s32[1024]{0:T(1024)S(1)} %get-tuple-element.48), kind=kCustom, calls=%fused_computation.3 | custom fusion | bytes 776192 | tf_op jit(solution)/shard_map/gather | solution.py:108
  113.1 2.2 %gather_fusion.2 = f32[512,189]{1,0:T(8,128)} fusion(f32[189,512]{0,1:T(8,128)S(1)} %copy.202, s32[1024]{0:T(1024)S(1)} %get-tuple-element.48), kind=kCustom, calls=%fused_computation.2 | custom fusion | bytes 776192 | tf_op jit(solution)/shard_map/gather | solution.py:108
  115.3 2.2 %gather_fusion.1 = f32[512,189]{1,0:T(8,128)} fusion(f32[189,512]{0,1:T(8,128)S(1)} %copy.199, s32[1024]{0:T(1024)S(1)} %get-tuple-element.48), kind=kCustom, calls=%fused_computation.1 | custom fusion | bytes 776192 | tf_op jit(solution)/shard_map/gather | solution.py:108
  117.6 2.2 %gather_fusion = f32[512,189]{1,0:T(8,128)} fusion(f32[189,512]{0,1:T(8,128)S(1)} %copy.196, s32[1024]{0:T(1024)S(1)} %get-tuple-element.48), kind=kCustom, calls=%fused_computation | custom fusion | bytes 776192 | tf_op jit(solution)/shard_map/gather | solution.py:108
  119.9 6.6 %gather_fusion.6 = s32[1024]{0:T(1024)S(1)} fusion(s32[128]{0:T(128)S(1)} %copy-done.1, s32[1024]{0:T(1024)S(1)} %get-tuple-element.49), kind=kCustom, calls=%fused_computation.6 | custom fusion | bytes 12288 | tf_op jit(solution)/shard_map/gather | solution.py:111
  127.3 0.9 convolution_bitcast_fusion
  128.6 1.0 scatter_custom_fusion.4
  129.7 0.8 reshape.215
  131.2 0.8 fusion.97
  132.1 2.2 %add_bitcast_fusion = f32[189,512]{0,1:T(8,128)S(1)} fusion(f32[512,189]{1,0:T(8,128)S(1)} %copy-done.17, f32[512,189]{1,0:T(8,128)} %gather_fusion.4, f32[512,189]{1,0:T(8,128)} %gather_fusion.3, f32[512,189]{1,0:T(8,128)} %gather_fusion.2, f32[512,189]{1,0:T(8,128)} %gather_fusion.1, f32[512,189]{1,0:T(8,128)} %gather_fusion, ...), kind=kLoop, calls=%fused_computation.52 | loop fusion | flops 1064448 | bytes 2721792 | tf_op jit(solution)/shard_map/add | solution.py:108
  134.3 1.4 fusion.64
  135.8 4.2 %collective-permute-done.1 = f32[6,189,256]{2,1,0:T(8,128)} collective-permute-done((f32[6,189,256]{2,1,0:T(8,128)}, f32[6,189,256]{2,1,0:T(8,128)}, u32[]{:S(2)}, u32[]{:S(2)}) %collective-permute-start.1) | collective-permute-done | bytes 1161248 | tf_op jit(solution)/shard_map/ppermute | solution.py:18
  140.1 1.4 fusion.52
  141.6 12.0 %collective-permute-done.2 = f32[6,189,256]{2,1,0:T(8,128)} collective-permute-done((f32[6,189,256]{2,1,0:T(8,128)}, f32[6,189,256]{2,1,0:T(8,128)}, u32[]{:S(2)}, u32[]{:S(2)}) %collective-permute-start.2) | collective-permute-done | bytes 1161248 | tf_op jit(solution)/shard_map/ppermute | solution.py:18
  153.7 1.4 fusion.40
  155.2 7.4 %collective-permute-done.3 = f32[6,189,256]{2,1,0:T(8,128)} collective-permute-done((f32[6,189,256]{2,1,0:T(8,128)}, f32[6,189,256]{2,1,0:T(8,128)}, u32[]{:S(2)}, u32[]{:S(2)}) %collective-permute-start.3) | collective-permute-done | bytes 1161248 | tf_op jit(solution)/shard_map/ppermute | solution.py:18
  162.6 1.4 fusion.28
  164.0 0.8 copy.227
  164.9 2.2 %scatter_fusion = f32[189,512]{0,1:T(8,128)S(1)} fusion(f32[189,512]{0,1:T(8,128)S(1)} %add_bitcast_fusion, s32[256]{0:T(256)S(1)} %bitcast.469, f32[256,189]{1,0:T(8,128)S(1)} %copy.224), kind=kCustom, calls=%fused_computation.13 | custom fusion | flops 48384 | bytes 581632 | tf_op jit(solution)/shard_map/scatter-add | solution.py:115
  167.1 2.2 %scatter_fusion.1 = f32[189,512]{0,1:T(8,128)S(1)} fusion(f32[189,512]{0,1:T(8,128)S(1)} %scatter_fusion, s32[256]{0:T(256)S(1)} %bitcast.468, f32[256,189]{1,0:T(8,128)S(1)} %copy.225), kind=kCustom, calls=%fused_computation.14 | custom fusion | flops 48384 | bytes 581632 | tf_op jit(solution)/shard_map/scatter-add | solution.py:115
  169.2 2.2 %scatter_fusion.2 = f32[189,512]{0,1:T(8,128)S(1)} fusion(f32[189,512]{0,1:T(8,128)S(1)} %scatter_fusion.1, s32[256]{0:T(256)S(1)} %bitcast.467, f32[256,189]{1,0:T(8,128)S(1)} %copy.226), kind=kCustom, calls=%fused_computation.15 | custom fusion | flops 48384 | bytes 581632 | tf_op jit(solution)/shard_map/scatter-add | solution.py:115
  171.4 2.2 %scatter_fusion.3 = f32[189,512]{0,1:T(8,128)S(1)} fusion(f32[189,512]{0,1:T(8,128)S(1)} %scatter_fusion.2, s32[256]{0:T(256)S(1)} %bitcast.466, f32[256,189]{1,0:T(8,128)S(1)} %copy-done.19), kind=kCustom, calls=%fused_computation.16 | custom fusion | flops 48384 | bytes 581632 | tf_op jit(solution)/shard_map/scatter-add | solution.py:115
  173.9 1.1 fusion
  175.2 1.2 fusion.1
  (120 shorter events, 12.5 us)
Async XLA Ops:
  0.0 1.0 copy-start
  2.8 6.1 %copy-start.12 = (f32[4,21,56]{2,0,1:T(4,128)S(1)}, f32[4,21,56]{2,0,1:T(4,128)}, u32[]{:S(2)}) copy-start(f32[4,21,56]{2,0,1:T(4,128)} %param.15) | copy-start | bytes 56452
  3.4 6.9 %copy-start.4 = (f32[9,56,128]{2,1,0:T(8,128)}, f32[9,56,128]{2,1,0:T(8,128)S(1)}, u32[]{:S(2)}) copy-start(f32[9,56,128]{2,1,0:T(8,128)S(1)} %multiply_reduce_fusion.5) | copy-start | bytes 774148
  5.0 6.5 %copy-start.6 = (f32[9,56,128]{2,1,0:T(8,128)}, f32[9,56,128]{2,1,0:T(8,128)S(1)}, u32[]{:S(2)}) copy-start(f32[9,56,128]{2,1,0:T(8,128)S(1)} %multiply_reduce_fusion.4) | copy-start | bytes 774148
  5.0 5.9 %copy-start.2 = (f32[9,56,128]{2,1,0:T(8,128)S(1)}, f32[9,56,128]{2,1,0:T(8,128)}, u32[]{:S(2)}) copy-start(f32[9,56,128]{2,1,0:T(8,128)} %param.12) | copy-start | bytes 774148
  6.5 6.3 %copy-start.8 = (f32[9,56,128]{2,1,0:T(8,128)}, f32[9,56,128]{2,1,0:T(8,128)S(1)}, u32[]{:S(2)}) copy-start(f32[9,56,128]{2,1,0:T(8,128)S(1)} %multiply_reduce_fusion.3) | copy-start | bytes 774148
  8.0 5.6 %copy-start.10 = (f32[9,56,128]{2,1,0:T(8,128)}, f32[9,56,128]{2,1,0:T(8,128)S(1)}, u32[]{:S(2)}) copy-start(f32[9,56,128]{2,1,0:T(8,128)S(1)} %multiply_reduce_fusion.2) | copy-start | bytes 774148
  12.1 1.5 copy-start.15
  19.2 6.5 %copy-start.23 = (s32[4,256]{1,0:T(4,128)S(1)}, s32[4,256]{1,0:T(4,128)}, u32[]{:S(2)}) copy-start(s32[4,256]{1,0:T(4,128)} %param.20) | copy-start | bytes 12292
  70.8 6.3 %copy-start.13 = (f32[4,256,189]{1,2,0:T(8,128)S(1)}, f32[4,256,189]{1,2,0:T(8,128)}, u32[]{:S(2)}) copy-start(f32[4,256,189]{1,2,0:T(8,128)} %copy.221) | copy-start | bytes 2322436
  70.8 7.3 %copy-start.14 = (f32[4,256,189]{1,2,0:T(8,128)S(1)}, f32[4,256,189]{1,2,0:T(8,128)}, u32[]{:S(2)}) copy-start(f32[4,256,189]{1,2,0:T(8,128)} %copy.223) | copy-start | bytes 2322436
  79.0 27.3 %copy-start.24 = (s32[4,128]{1,0:T(4,128)S(1)}, s32[4,128]{1,0:T(4,128)}, u32[]{:S(2)}) copy-start(s32[4,128]{1,0:T(4,128)} %param.19) | copy-start | bytes 6148
  79.0 27.3 %copy-start.20 = (s32[4,256]{1,0:T(4,128)S(1)}, s32[4,256]{1,0:T(4,128)}, u32[]{:S(2)}) copy-start(s32[4,256]{1,0:T(4,128)} %param.21) | copy-start | bytes 12292
  83.7 50.5 %collective-permute-start = (f32[6,189,256]{2,1,0:T(8,128)}, f32[6,189,256]{2,1,0:T(8,128)}, u32[]{:S(2)}, u32[]{:S(2)}) collective-permute-start(f32[6,189,256]{2,1,0:T(8,128)} %get-tuple-element.10), channel_id=1, source_target_pairs={{0,12},{12,24},{24,36},{36,48},{48,60},{60,72},{72,84},{84,96},{96... | collective-permute-start | bytes 3483656 | tf_op jit(solution)/shard_map/ppermute | solution.py:18
  85.7 54.4 %collective-permute-start.1 = (f32[6,189,256]{2,1,0:T(8,128)}, f32[6,189,256]{2,1,0:T(8,128)}, u32[]{:S(2)}, u32[]{:S(2)}) collective-permute-start(f32[6,189,256]{2,1,0:T(8,128)} %get-tuple-element.9), channel_id=1, source_target_pairs={{12,0},{24,12},{36,24},{48,36},{60,48},{72,60},{84,72},{96,84},{10... | collective-permute-start | bytes 3483656 | tf_op jit(solution)/shard_map/ppermute | solution.py:18
  100.5 53.2 %collective-permute-start.2 = (f32[6,189,256]{2,1,0:T(8,128)}, f32[6,189,256]{2,1,0:T(8,128)}, u32[]{:S(2)}, u32[]{:S(2)}) collective-permute-start(f32[6,189,256]{2,1,0:T(8,128)} %get-tuple-element.8), channel_id=1, source_target_pairs={{0,1},{1,2},{2,3},{3,4},{4,5},{5,6},{6,7},{7,8},{8,9},{9,10},{10,1... | collective-permute-start | bytes 3483656 | tf_op jit(solution)/shard_map/ppermute | solution.py:18
  103.8 58.8 %collective-permute-start.3 = (f32[6,189,256]{2,1,0:T(8,128)}, f32[6,189,256]{2,1,0:T(8,128)}, u32[]{:S(2)}, u32[]{:S(2)}) collective-permute-start(f32[6,189,256]{2,1,0:T(8,128)} %get-tuple-element.7), channel_id=1, source_target_pairs={{1,0},{2,1},{3,2},{4,3},{5,4},{6,5},{7,6},{8,7},{9,8},{10,9},{11,1... | collective-permute-start | bytes 3483656 | tf_op jit(solution)/shard_map/ppermute | solution.py:18
  113.1 6.7 %copy-start.1 = (s32[128]{0:T(128)S(1)}, s32[128]{0:T(128)}, u32[]{:S(2)}) copy-start(s32[128]{0:T(128)} %param.18) | copy-start | bytes 1540
  117.6 9.0 %copy-start.3 = (f32[9,56,128]{2,1,0:T(8,128)S(1)}, f32[9,56,128]{2,1,0:T(8,128)}, u32[]{:S(2)}) copy-start(f32[9,56,128]{2,1,0:T(8,128)} %param.12) | copy-start | bytes 774148
  117.6 9.0 %copy-start.5 = (f32[9,56,128]{2,1,0:T(8,128)S(1)}, f32[9,56,128]{2,1,0:T(8,128)}, u32[]{:S(2)}) copy-start(f32[9,56,128]{2,1,0:T(8,128)} %copy-done.4) | copy-start | bytes 774148
  117.6 9.0 %copy-start.7 = (f32[9,56,128]{2,1,0:T(8,128)S(1)}, f32[9,56,128]{2,1,0:T(8,128)}, u32[]{:S(2)}) copy-start(f32[9,56,128]{2,1,0:T(8,128)} %copy-done.6) | copy-start | bytes 774148
  117.6 9.0 %copy-start.9 = (f32[9,56,128]{2,1,0:T(8,128)S(1)}, f32[9,56,128]{2,1,0:T(8,128)}, u32[]{:S(2)}) copy-start(f32[9,56,128]{2,1,0:T(8,128)} %copy-done.8) | copy-start | bytes 774148
  117.6 9.0 %copy-start.11 = (f32[9,56,128]{2,1,0:T(8,128)S(1)}, f32[9,56,128]{2,1,0:T(8,128)}, u32[]{:S(2)}) copy-start(f32[9,56,128]{2,1,0:T(8,128)} %copy-done.10) | copy-start | bytes 774148
  117.6 9.0 %copy-start.16 = (f32[9,56,128]{2,1,0:T(8,128)S(1)}, f32[9,56,128]{2,1,0:T(8,128)}, u32[]{:S(2)}) copy-start(f32[9,56,128]{2,1,0:T(8,128)} %copy-done.15) | copy-start | bytes 774148
  119.9 8.7 %copy-start.25 = (s32[64]{0:T(128)S(1)}, s32[64]{0:T(128)}, u32[]{:S(2)}) copy-start(s32[64]{0:T(128)} %param.22) | copy-start | bytes 772
  119.9 8.7 %copy-start.26 = (s32[64]{0:T(128)S(1)}, s32[64]{0:T(128)}, u32[]{:S(2)}) copy-start(s32[64]{0:T(128)} %param.23) | copy-start | bytes 772
  126.5 4.7 %copy-start.21 = (f32[9,9]{1,0:T(8,128)S(1)}, f32[9,9]{1,0:T(8,128)}, u32[]{:S(2)}) copy-start(f32[9,9]{1,0:T(8,128)} %param.16) | copy-start | bytes 976
  126.6 5.5 %copy-start.17 = (f32[512,189]{1,0:T(8,128)S(1)}, f32[512,189]{1,0:T(8,128)}, u32[]{:S(2)}) copy-start(f32[512,189]{1,0:T(8,128)} %gather_fusion.5) | copy-start | bytes 1161220
  167.0 4.4 %copy-start.19 = (f32[256,189]{1,0:T(8,128)S(1)}, f32[256,189]{1,0:T(8,128)}, u32[]{:S(2)}) copy-start(f32[256,189]{1,0:T(8,128)} %copy.227) | copy-start | bytes 580612
  167.0 6.8 %copy-start.18 = (f32[189,512]{1,0:T(8,128)S(1)}, f32[189,512]{1,0:T(8,128)}, u32[]{:S(2)}) copy-start(f32[189,512]{1,0:T(8,128)} %reshape.215) | copy-start | bytes 1161220
  169.2 4.7 %copy-start.22 = (f32[9,9]{1,0:T(8,128)S(1)}, f32[9,9]{1,0:T(8,128)}, u32[]{:S(2)}) copy-start(f32[9,9]{1,0:T(8,128)} %param.17) | copy-start | bytes 976
where the time goes:
time: 177 us; the launch traced here: 176 us
  local copies, waits for them, and re-layouts  95.7 us (54%)
  waiting for transfers between devices  23.6 us (13%)
  starting transfers between devices  22.6 us (13%)
  other arithmetic  20.9 us (12%)
  matrix products  12.5 us (7%)
    gather x12, local copies, waits for them, and re-layouts, shards(): sent.append(faces[:, send_slots])  43 us
    ppermute x4, waiting for transfers between devices, shifted(): lax.ppermute(value, axis, [(source, source + steps) for source in range(f...  23.6 us
    ppermute x4, starting transfers between devices, shifted(): lax.ppermute(value, axis, [(source, source + steps) for source in range(f...  22.6 us
    unnamed x74, local copies, waits for them, and re-layouts  15.4 us
    gather x6, local copies, waits for them, and re-layouts, shards(): faces[:, flat_neighbour]  13.4 us
    scatter-add x4, other arithmetic, shards(): outer = outer.at[:, receive_slots[direction]].add(arrived)  8.68 us
    reshape x6, local copies, waits for them, and re-layouts, on_faces(): return faces.reshape(FIELDS * FACE_MODES, -1)  7.31 us
    gather x1, local copies, waits for them, and re-layouts, shards(): target_level = rate_level[receive_slots % count]  6.57 us
  transfers between devices with their start and end apart: 4, of which 3 were waited for; matrix products, arithmetic and copies ran while one was open for 18% of the time, Pallas kernels for 0%

commit v1 on v0

v1 whole, which is shorter than its diff:
```python
import functools

import jax
import jax.numpy as jnp
from jax import lax
from jax.experimental import pallas as pl
from jax.experimental.pallas import tpu as pltpu
from jax.sharding import PartitionSpec as P

FIELDS = 9
MODES = 56
FACE_MODES = 21
ORDER = 6
LEVELS = 3
COUNT = 128
SLOTS = 256
ROWS = FIELDS * FACE_MODES

coarse_dt = 2.0
slip_keep = 0.3

f32 = jnp.float32
bf16 = jnp.bfloat16


def level_terms(level):
    step = coarse_dt * 2.0**-level
    terms = []
    factor = step
    for degree in range(ORDER):
        terms.append(factor)
        factor = factor * step / (degree + 2.0)
    return terms


def split(value):
    high = value.astype(bf16)
    low = (value - high.astype(f32)).astype(bf16)
    return high, low


def split_f32(value):
    high = value.astype(bf16).astype(f32)
    return high, value - high


def matmul(left, right):
    return jnp.dot(left, right, preferred_element_type=f32)


def matmul_nt(left, right):
    return lax.dot_general(left, right, (((1,), (1,)), ((), ())), preferred_element_type=f32)


def place_triple(ref, row, value):
    rows, cols = value.shape
    high, low = split_f32(value)
    for slot, part in enumerate((high, high, low)):
        ref[row : row + rows, slot * 64 : slot * 64 + cols] = part


def element_hot(faces, count):
    which = lax.broadcasted_iota(jnp.int32, (COUNT, count), 0)
    return jnp.where(which == (faces & (COUNT - 1)), 1.0, 0.0).astype(bf16)


def block_hot(hot, blocks, block):
    mask = jnp.where(blocks == block, 1.0, 0.0)
    return hot * jnp.broadcast_to(mask, hot.shape).astype(bf16)


def pair_row(ref):
    return jnp.concatenate([ref[0:1, :], ref[1:2, :]], axis=1)


def fill_modal(modal, left, pieces):
    for first in range(0, FIELDS * COUNT, 2 * COUNT):
        columns = slice(first, min(first + 2 * COUNT, FIELDS * COUNT))
        right = jnp.concatenate([pieces[:, columns], pieces[0:64, columns]], axis=0)
        modal[:, columns] = matmul(left[...], right)


def mix_star(modal, star, group):
    sums = [None] * len(group)
    for d in range(3):
        for q in range(FIELDS):
            value = modal[d * MODES : (d + 1) * MODES, q * COUNT : (q + 1) * COUNT]
            for at, p in enumerate(group):
                term = star[q, p, d : d + 1, :] * value
                sums[at] = term if sums[at] is None else sums[at] + term
    return sums


def levels_kernel(
    odd, level_in, receive_in, send_in, stiffness_in, faces_in, neighbour_in, fault_in, flags_in, inner_in, outer_in,
    state_in, star_in,
    level, receive, send, stiffness, face_project, neighbour, fault, flags, flux_inner, flux_outer,
    state, star,
    level_a, level_c, want_b, want_d,
    receive_all, send_all, faces_all, inner_all, outer_all, square, sems,
):
    ends = (
        (level_in, level), (receive_in, receive_all), (send_in, send_all), (stiffness_in, stiffness),
        (faces_in, faces_all), (neighbour_in, neighbour), (fault_in, fault), (flags_in, flags), (inner_in, inner_all),
        (outer_in, outer_all), (state_in, state), (star_in, star),
    )
    moves = [pltpu.make_async_copy(source, copy, sems.at[at]) for at, (source, copy) in enumerate(ends)]
    for move in moves:
        move.start()
    odd_x, odd_y = odd[0:1, :] == 1, odd[1:2, :] == 1
    for at in range(3):
        moves[at].wait()
    level_all = jnp.broadcast_to(level[...], (8, COUNT))
    rows = []
    coming = [receive_all[at : at + 1, :] for at in range(4)]
    going = [send_all[at : at + 1, :] for at in range(4)]
    for at, (flip, first) in enumerate(((odd_x, 0), (odd_y, 2))):
        one, other = first, first + 1
        send[at : at + 1, :] = jnp.where(flip, going[other], going[one])
        send[at + 2 : at + 3, :] = jnp.where(flip, going[one], going[other])
        receive[at : at + 1, :] = jnp.where(flip, coming[one], coming[other])
        receive[at + 2 : at + 3, :] = jnp.where(flip, coming[other], coming[one])
    for at in range(4):
        row = receive[at : at + 1, :]
        rows += [row[:, :COUNT], row[:, COUNT:]]
    index = jnp.concatenate(rows, axis=0) & (COUNT - 1)
    found = jnp.take_along_axis(level_all, index, axis=1, mode="promise_in_bounds")
    for at, out in enumerate((level_a, level_c, want_b, want_d)):
        out[...] = found[2 * at : 2 * at + 2, :]
    for at in range(3, 5):
        moves[at].wait()
    for f in range(4):
        face_project[f] = faces_all[:, f, :]
    for at in range(5, 10):
        moves[at].wait()
    for source, spread in ((inner_all, flux_inner), (outer_all, flux_outer)):
        square[...] = jnp.zeros_like(square)
        square[0:FIELDS, 0:FIELDS] = source[...]
        turned = square[...].T
        for q in range(FIELDS):
            spread[q] = jnp.broadcast_to(turned[0:FIELDS, q : q + 1], (FIELDS, COUNT))
    for at in range(10, len(moves)):
        moves[at].wait()


def taylor_kernel(
    state, star, stiffness, face_project, level,
    table, own,
    wide, left, face_left, stack, modal, pieces, level_pieces,
):
    wide[...] = jnp.zeros_like(wide)
    for d in range(3):
        place_triple(wide, d * MODES, -stiffness[d])
    left[...] = wide[0:168, 0:192].astype(bf16)
    wide[0:96, :] = jnp.zeros((96, 256), f32)
    for f in range(4):
        place_triple(wide, f * 24, face_project[f])
    face_left[...] = wide[0:96, 0:192].astype(bf16)
    pieces[...] = jnp.zeros_like(pieces)
    level_pieces[...] = jnp.zeros_like(level_pieces)

    for q in range(FIELDS):
        value = state[q]
        stack[0, q] = value
        high, low = split(value)
        pieces[0:MODES, q * COUNT : (q + 1) * COUNT] = high
        pieces[64 : 64 + MODES, q * COUNT : (q + 1) * COUNT] = low

    def step(degree, carry):
        fill_modal(modal, left, pieces)
        for first in range(0, FIELDS, 3):
            group = range(first, first + 3)
            for p, value in zip(group, mix_star(modal, star, group)):
                stack[degree + 1, p] = value
                high, low = split(value)
                pieces[0:MODES, p * COUNT : (p + 1) * COUNT] = high
                pieces[64 : 64 + MODES, p * COUNT : (p + 1) * COUNT] = low
        return carry

    lax.fori_loop(0, ORDER - 1, step, 0)

    terms = [level_terms(at) for at in range(LEVELS)]
    for q in range(FIELDS):
        sums = [None] * LEVELS
        for degree in range(ORDER):
            value = stack[degree, q]
            for at in range(LEVELS):
                term = terms[at][degree] * value
                sums[at] = term if degree == 0 else sums[at] + term
        own[q] = jnp.where(level[...] == 0, sums[0], jnp.where(level[...] == 1, sums[1], sums[2]))
        for at in range(LEVELS):
            high, low = split(sums[at])
            column = (at * FIELDS + q) * COUNT
            level_pieces[0:MODES, column : column + COUNT] = high
            level_pieces[64 : 64 + MODES, column : column + COUNT] = low

    for at in range(LEVELS):
        columns = slice(at * FIELDS * COUNT, (at + 1) * FIELDS * COUNT)
        right = jnp.concatenate([level_pieces[:, columns], level_pieces[0:64, columns]], axis=0)
        faces = matmul(face_left[...], right)
        for q in range(FIELDS):
            for f in range(4):
                high, low = split_f32(faces[f * 24 : f * 24 + 24, q * COUNT : (q + 1) * COUNT])
                column = (at * 4 + f) * COUNT
                table[q * 48 : q * 48 + 48, column : column + COUNT] = jnp.concatenate(
                    [high, low], axis=0
                ).astype(bf16)


def put(out, found):
    for q in range(FIELDS):
        both = found[q * 48 : q * 48 + 24, :] + found[q * 48 + 24 : q * 48 + 48, :]
        out[q * FACE_MODES : (q + 1) * FACE_MODES, :] = both[:FACE_MODES, :]


def gather_slots(faces, levels, table, out, hot):
    blocks = levels * 4 + (faces >> 7)
    element = element_hot(faces, SLOTS)
    for block in range(12):
        hot[block * COUNT : (block + 1) * COUNT, :] = block_hot(element, blocks, block)
    put(out, matmul(table[...], hot[...]))


def gather_kernel(at, send, levels, table, out, hot):
    gather_slots(send[at : at + 1, :], pair_row(levels), table, out, hot)


def gather_levels_kernel(at, send, table, out, hot):
    faces = send[at : at + 1, :]
    element = element_hot(faces, SLOTS)
    for block in range(4):
        hot[block * COUNT : (block + 1) * COUNT, :] = block_hot(element, faces >> 7, block)
    for level in range(LEVELS):
        put(out.at[level], matmul(table[:, level * 512 : level * 512 + 512], hot[...]))


def face_transposed(square, face_project):
    square[...] = jnp.zeros_like(square)
    for f in range(4):
        square[f * 24 : f * 24 + FACE_MODES, 0:MODES] = face_project[f]
    return square[...].T[0:MODES, 0:96]


def local_kernel(
    flux_inner, state, star, stiffness, face_project, level, neighbour, fault, flags, receive, table, own,
    base, outer, keep, lift_left, arrive_hot,
    square, wide, left, pieces, modal, hot,
):
    projected = face_transposed(square, face_project)
    rows = square[0:96, :]
    high, low = split(projected)
    lift_left[:, 0:96] = high.astype(f32)
    lift_left[:, 96:192] = high.astype(f32)
    lift_left[:, 192:288] = low.astype(f32)
    right_high, right_low = split(rows)
    gram = (
        matmul(high, right_high) + matmul(high, right_low) + matmul(low, right_high)
    )[:, 0:MODES]
    wide[...] = jnp.zeros_like(wide)
    place_triple(wide, 3 * MODES, gram)
    square[...] = jnp.zeros_like(square)
    for d in range(3):
        square[0:MODES, 0:MODES] = stiffness[d]
        place_triple(wide, d * MODES, square[...].T[0:MODES, 0:MODES])
    left[...] = wide[0:224, 0:192].astype(bf16)
    pieces[...] = jnp.zeros_like(pieces)
    for q in range(FIELDS):
        high, low = split(own[q])
        pieces[0:MODES, q * COUNT : (q + 1) * COUNT] = high
        pieces[64 : 64 + MODES, q * COUNT : (q + 1) * COUNT] = low
    fill_modal(modal, left, pieces)
    for first in range(0, FIELDS, 3):
        group = range(first, first + 3)
        sums = mix_star(modal, star, group)
        for q in range(FIELDS):
            value = modal[168:224, q * COUNT : (q + 1) * COUNT]
            for at, p in enumerate(group):
                sums[at] = sums[at] + flux_inner[q, p : p + 1, :] * value
        for at, p in enumerate(group):
            base[p] = state[p] + sums[at]

    for f in range(4):
        faces = neighbour[f : f + 1, :]
        blocks = level[...] * 4 + (faces >> 7)
        element = element_hot(faces, COUNT)
        for block in range(12):
            hot[block * COUNT : (block + 1) * COUNT, f * COUNT : (f + 1) * COUNT] = block_hot(
                element, blocks, block
            )
    found = matmul(table[...], hot[...])
    for q in range(FIELDS):
        outer[q * 24 : q * 24 + 24, :] = found[q * 48 : q * 48 + 24, :] + found[q * 48 + 24 : q * 48 + 48, :]

    which = lax.broadcasted_iota(jnp.int32, (4 * COUNT, fault.shape[1]), 0)
    at_fault = jnp.where(which == fault[...], 1.0, 0.0).astype(bf16)
    slips = jnp.broadcast_to(flags[...].astype(f32), (16, fault.shape[1])).astype(bf16)
    keep[...] = 1.0 - (1.0 - slip_keep) * matmul_nt(slips, at_fault)[0:8, :]

    for at in range(4):
        faces = receive[at : at + 1, :]
        element = element_hot(faces, SLOTS)
        for block in range(4):
            arrive_hot[block * COUNT : (block + 1) * COUNT, at * SLOTS : (at + 1) * SLOTS] = block_hot(
                element, faces >> 7, block
            )


def place_arrived(arrived, at, pick):
    for q in range(FIELDS):
        value = pick(slice(q * FACE_MODES, (q + 1) * FACE_MODES))
        value = jnp.concatenate([value, jnp.zeros((3, SLOTS), f32)], axis=0)
        high, low = split_f32(value)
        arrived[q * 48 : q * 48 + 48, at * SLOTS : (at + 1) * SLOTS] = jnp.concatenate([high, low], axis=0).astype(
            bf16
        )


def picked(levels, arrive, rows):
    return jnp.where(levels == 0, arrive[0, rows, :], jnp.where(levels == 1, arrive[1, rows, :], arrive[2, rows, :]))


def absorb_kernel(level_a, level_c, arrive_a, arrive_c, arrive_hot, outer, total, arrived):
    for at, (level, arrive) in enumerate(((level_a, arrive_a), (level_c, arrive_c))):
        levels = pair_row(level)
        place_arrived(arrived, at, lambda rows: picked(levels, arrive, rows))
    found = matmul_nt(arrived[...], arrive_hot[:, 0:512])
    for q in range(FIELDS):
        total[q * 24 : q * 24 + 24, :] = (
            outer[q * 24 : q * 24 + 24, :] + found[q * 48 : q * 48 + 24, :] + found[q * 48 + 24 : q * 48 + 48, :]
        )


def final_kernel(
    flux_outer, arrive_b, arrive_d, arrive_hot, base, outer, keep, lift_left,
    updated,
    arrived, lifted_right, lifted,
):
    place_arrived(arrived, 0, lambda rows: arrive_b[rows, :])
    place_arrived(arrived, 1, lambda rows: arrive_d[rows, :])
    found = matmul_nt(arrived[...], arrive_hot[:, 512:1024])
    for q in range(FIELDS):
        total = found[q * 48 : q * 48 + 24, :] + found[q * 48 + 24 : q * 48 + 48, :] + outer[q * 24 : q * 24 + 24, :]
        if 3 <= q < 6:
            total = total * keep[0:1, :]
        faces = jnp.concatenate([total[:, f * COUNT : (f + 1) * COUNT] for f in range(4)], axis=0)
        high, low = split(faces)
        columns = slice(q * COUNT, (q + 1) * COUNT)
        lifted_right[0:96, columns] = high
        lifted_right[96:192, columns] = low
        lifted_right[192:288, columns] = high
    left = lift_left[...].astype(bf16)
    for first in range(0, FIELDS * COUNT, 2 * COUNT):
        columns = slice(first, min(first + 2 * COUNT, FIELDS * COUNT))
        lifted[:, columns] = matmul(left, lifted_right[:, columns])
    for first in range(0, FIELDS, 3):
        sums = [base[p] for p in range(first, first + 3)]
        for q in range(FIELDS):
            value = lifted[:, q * COUNT : (q + 1) * COUNT]
            for at in range(3):
                sums[at] = sums[at] + flux_outer[q, first + at : first + at + 1, :] * value
        for at in range(3):
            updated[first + at] = sums[at]


def spec(space=pltpu.VMEM):
    return pl.BlockSpec(memory_space=space)


def call(kernel, outs, scratch, near, values, flops, space=pltpu.VMEM):
    moved = sum(4 * value.size for value in values)
    if space is pltpu.HBM:
        values = [pltpu.with_memory_space_constraint(value, space) for value in values]
    return pl.pallas_call(
        kernel,
        out_shape=outs,
        in_specs=[spec()] * len(near) + [spec(space)] * len(values),
        out_specs=jax.tree.map(lambda _: spec(), outs),
        scratch_shapes=scratch,
        cost_estimate=pl.CostEstimate(flops=flops, bytes_accessed=moved, transcendentals=0),
        compiler_params=pltpu.CompilerParams(vmem_limit_bytes=24 << 20),
    )(*near, *values)


def shape(*dims, dtype=f32):
    return jax.ShapeDtypeStruct(dims, dtype)


def swapped(value, axis, first):
    count = lax.axis_size(axis)
    pairs = []
    for low in range(first, count - 1, 2):
        pairs += [(low, low + 1), (low + 1, low)]
    return lax.ppermute(value, axis, pairs)


def shards(
    state, star_matrices, stiffness, face_project, flux_inner, flux_outer, rate_level, neighbour,
    send_slots, receive_slots, fault_faces, slip_flags,
):
    along = lax.broadcasted_iota(jnp.int32, (8, SLOTS), 0)
    odd = jnp.where(along == 0, lax.axis_index("gx") & 1, lax.axis_index("gy") & 1)
    inputs = (
        rate_level.reshape(1, COUNT), receive_slots, send_slots, stiffness, face_project.transpose(1, 0, 2), neighbour,
        fault_faces.reshape(1, -1), slip_flags.reshape(1, -1), flux_inner, flux_outer, state, star_matrices.transpose(1, 2, 0, 3),
    )
    held = [shape(*value.shape, dtype=value.dtype) for value in inputs]
    held[4] = shape(*face_project.shape)
    held[8] = held[9] = shape(FIELDS, FIELDS, COUNT)
    row = shape(2, COUNT, dtype=jnp.int32)
    level, receive, send, stiffness, face_project, neighbour, fault, flags, *rest = call(
        levels_kernel,
        tuple(held) + (row,) * 4,
        [
            pltpu.VMEM(receive_slots.shape, jnp.int32),
            pltpu.VMEM(send_slots.shape, jnp.int32),
            pltpu.VMEM(inputs[4].shape, f32),
            pltpu.VMEM((FIELDS, FIELDS), f32),
            pltpu.VMEM((FIELDS, FIELDS), f32),
            pltpu.VMEM((128, 128), f32),
            pltpu.SemaphoreType.DMA((len(inputs),)),
        ],
        (odd,), inputs, 1000, pltpu.HBM,
    )
    flux_inner, flux_outer, state, star, level_a, level_c, want_b, want_d = rest
    level_b = swapped(want_b, "gx", 1)
    level_d = swapped(want_d, "gy", 1)

    table, own = call(
        taylor_kernel,
        (shape(FIELDS * 48, LEVELS * 4 * COUNT, dtype=bf16), shape(FIELDS, MODES, COUNT)),
        [
            pltpu.VMEM((224, 256), f32),
            pltpu.VMEM((168, 192), bf16),
            pltpu.VMEM((96, 192), bf16),
            pltpu.VMEM((ORDER, FIELDS, MODES, COUNT), f32),
            pltpu.VMEM((168, FIELDS * COUNT), f32),
            pltpu.VMEM((128, FIELDS * COUNT), bf16),
            pltpu.VMEM((128, LEVELS * FIELDS * COUNT), bf16),
        ],
        (),
        (state, star, stiffness, face_project, level),
        2000000000,
    )
    piece, pieces = shape(ROWS, SLOTS), shape(LEVELS, ROWS, SLOTS)

    def gathered(at, levels):
        return call(
            functools.partial(gather_kernel, at), piece, [pltpu.VMEM((LEVELS * 4 * COUNT, SLOTS), bf16)], (),
            (send, levels, table), 300000000,
        )

    def gathered_levels(at):
        return call(
            functools.partial(gather_levels_kernel, at), pieces, [pltpu.VMEM((4 * COUNT, SLOTS), bf16)], (),
            (send, table), 300000000,
        )

    arrive_b = swapped(gathered(2, level_b), "gx", 1)
    arrive_c = swapped(gathered_levels(1), "gy", 0)
    arrive_d = swapped(gathered(3, level_d), "gy", 1)
    arrive_a = swapped(gathered_levels(0), "gx", 0)

    base, outer, keep, lift_left, arrive_hot = call(
        local_kernel,
        (
            shape(FIELDS, MODES, COUNT), shape(FIELDS * 24, 4 * COUNT), shape(8, 4 * COUNT), shape(MODES, 288),
            shape(4 * COUNT, 4 * SLOTS, dtype=bf16),
        ),
        [
            pltpu.VMEM((128, 128), f32),
            pltpu.VMEM((224, 256), f32),
            pltpu.VMEM((224, 192), bf16),
            pltpu.VMEM((128, FIELDS * COUNT), bf16),
            pltpu.VMEM((224, FIELDS * COUNT), f32),
            pltpu.VMEM((LEVELS * 4 * COUNT, 4 * COUNT), bf16),
        ],
        (),
        (flux_inner, state, star, stiffness, face_project, level, neighbour, fault, flags, receive, table, own),
        1000000000,
    )
    arrived = pltpu.VMEM((FIELDS * 48, 2 * SLOTS), bf16)
    outer = call(
        absorb_kernel, shape(FIELDS * 24, 4 * COUNT), [arrived], (),
        (level_a, level_c, arrive_a, arrive_c, arrive_hot, outer), 300000000,
    )
    return call(
        final_kernel,
        shape(FIELDS, MODES, COUNT),
        [arrived, pltpu.VMEM((288, FIELDS * COUNT), bf16), pltpu.VMEM((MODES, FIELDS * COUNT), f32)],
        (),
        (flux_outer, arrive_b, arrive_d, arrive_hot, base, outer, keep, lift_left),
        500000000,
    )


def solution(mesh):
    placed = (
        P(None, None, ("gx", "gy")),
        P(None, None, None, ("gx", "gy")),
        P(),
        P(),
        P(),
        P(),
        P(("gx", "gy")),
        P(None, ("gx", "gy")),
        P(None, ("gx", "gy")),
        P(None, ("gx", "gy")),
        P(("gx", "gy")),
        P(("gx", "gy")),
    )

    return jax.shard_map(shards, mesh=mesh, in_specs=placed, out_specs=P(None, None, ("gx", "gy")), check_vma=False)
```

time: 177 us -> 49.7 us (0.28)
  the two profiles are of different devices: /device:TPU:54 before, /device:TPU:96 now
where the time goes in v1:
time: 49.7 us; the launch traced here: 49.4 us
  starting transfers between devices  32.7 us (66%)
  Pallas kernels  12.8 us (26%)
  waiting for transfers between devices  3.73 us (8%)
    ppermute x6, starting transfers between devices, swapped(): return lax.ppermute(value, axis, pairs)  32.7 us
    pallas_call x9, Pallas kernels, call(): pl.pallas_call(kernel, out_shape=outs, in_specs=[spec()] * len(near) + [s...  12.8 us
    ppermute x6, waiting for transfers between devices, swapped(): return lax.ppermute(value, axis, pairs)  3.73 us
  transfers between devices with their start and end apart: 6, of which 2 were waited for; matrix products, arithmetic and copies ran while one was open for 0% of the time, Pallas kernels for 9%

profile of v1, /device:TPU:96, one launch (start us, length us, event | category | flops | bytes accessed | tf_op | source)
XLA Modules:
  0.0 49.4 jit_solution(4547283969402055615)
XLA Ops:
  0.0 0.1 iota.7.odd
  0.1 1.3 %shard_map.118 = (s32[1,128]{1,0:T(1,128)S(1)}, s32[4,256]{1,0:T(4,128)S(1)}, s32[4,256]{1,0:T(4,128)S(1)}, f32[3,56,56]{2,1,0:T(8,128)S(1)}, f32[4,21,56]{2,1,0...) custom-call(s32[8,256]{1,0:T(8,128)S(1)} %iota.7.odd, ...), custom_call_target="tpu_custom_call" | custom-call | flops 1000 | bytes 450824 | tf_op jit(solution)/shard_map/pallas_call | solution.py:373
  1.4 5.1 %shard_map.119 = (bf16[432,1536]{1,0:T(8,128)(2,1)S(1)}, f32[9,56,128]{2,1,0:T(8,128)S(1)}) custom-call(f32[9,56,128]{2,1,0:T(8,128)S(1)} %get-tuple-element.31.state, f32[9,9,3,128]{3,2,1,0:T(4,128)S(1)} %get-tuple-element.32.star, f32[3,56,56]{2,1,0:T(8,128)S(1)} %get-tuple-element.33.stiffness, f32[4,21,56]{2,1,0:T(8,128)S(1)} %get-tuple-element.34.face_project, ...), custom_call_target="tpu_custom_call" | custom-call | flops 2000000000 | bytes 439424 | tf_op jit(solution)/shard_map/pallas_call | solution.py:373
  6.5 0.5 %shard_map.123 = f32[3,189,256]{2,1,0:T(8,128)S(1)} custom-call(s32[4,256]{1,0:T(4,128)S(1)} %get-tuple-element.29.send, bf16[432,1536]{1,0:T(8,128)(2,1)S(1)} %get-tuple-element.36.table), custom_call_target="tpu_custom_call" | custom-call | flops 300000000 | bytes 2658304 | tf_op jit(solution)/shard_map/pallas_call | solution.py:373
  7.1 1.9 %collective-permute-start.4 = (f32[3,189,256]{2,1,0:T(8,128)S(1)}, f32[3,189,256]{2,1,0:T(8,128)S(1)}, u32[]{:S(2)}, u32[]{:S(2)}) collective-permute-start(f32[3,189,256]{2,1,0:T(8,128)S(1)} %shard_map.123), channel_id=1, source_target_pairs={{0,12},{12,0},{24,36},{36,24},{48,60},{60,48},{72,84},{84,72},{96,... | collective-permute-start | bytes 1741832 | tf_op jit(solution)/shard_map/ppermute | solution.py:393
  9.0 0.5 %shard_map.124 = f32[3,189,256]{2,1,0:T(8,128)S(1)} custom-call(s32[4,256]{1,0:T(4,128)S(1)} %get-tuple-element.29.send, bf16[432,1536]{1,0:T(8,128)(2,1)S(1)} %get-tuple-element.36.table), custom_call_target="tpu_custom_call" | custom-call | flops 300000000 | bytes 2658304 | tf_op jit(solution)/shard_map/pallas_call | solution.py:373
  9.5 3.4 %collective-permute-start.5 = (f32[3,189,256]{2,1,0:T(8,128)S(1)}, f32[3,189,256]{2,1,0:T(8,128)S(1)}, u32[]{:S(2)}, u32[]{:S(2)}) collective-permute-start(f32[3,189,256]{2,1,0:T(8,128)S(1)} %shard_map.124), channel_id=1, source_target_pairs={{0,1},{1,0},{2,3},{3,2},{4,5},{5,4},{6,7},{7,6},{8,9},{9,8},{10,11... | collective-permute-start | bytes 1741832 | tf_op jit(solution)/shard_map/ppermute | solution.py:393
  12.9 13.4 %collective-permute-start = (s32[2,128]{1,0:T(2,128)S(1)}, s32[2,128]{1,0:T(2,128)S(1)}, u32[]{:S(2)}, u32[]{:S(2)}) collective-permute-start(s32[2,128]{1,0:T(2,128)S(1)} %get-tuple-element.30), channel_id=1, source_target_pairs={{12,24},{24,12},{36,48},{48,36},{60,72},{72,60},{84,96},{96,84},{1... | collective-permute-start | bytes 3080 | tf_op jit(solution)/shard_map/ppermute | solution.py:393
  26.3 4.0 %collective-permute-start.2 = (s32[2,128]{1,0:T(2,128)S(1)}, s32[2,128]{1,0:T(2,128)S(1)}, u32[]{:S(2)}, u32[]{:S(2)}) collective-permute-start(s32[2,128]{1,0:T(2,128)S(1)} %get-tuple-element.37), channel_id=1, source_target_pairs={{1,2},{2,1},{3,4},{4,3},{5,6},{6,5},{7,8},{8,7},{9,10},{10,9},{13,... | collective-permute-start | bytes 3080 | tf_op jit(solution)/shard_map/ppermute | solution.py:393
  30.3 0.0 collective-permute-done.levels
  30.3 0.5 %shard_map.120 = f32[189,256]{1,0:T(8,128)S(1)} custom-call(s32[4,256]{1,0:T(4,128)S(1)} %get-tuple-element.29.send, s32[2,128]{1,0:T(2,128)S(1)} %collective-permute-done.levels, bf16[432,1536]{1,0:T(8,128)(2,1)S(1)} %get-tuple-element.36.table), custom_call_target="tpu_custom_call" | custom-call | flops 300000000 | bytes 2659328 | tf_op jit(solution)/shard_map/pallas_call | solution.py:373
  30.8 6.1 %collective-permute-start.1 = (f32[189,256]{1,0:T(8,128)S(1)}, f32[189,256]{1,0:T(8,128)S(1)}, u32[]{:S(2)}, u32[]{:S(2)}) collective-permute-start(f32[189,256]{1,0:T(8,128)S(1)} %shard_map.120), channel_id=1, source_target_pairs={{12,24},{24,12},{36,48},{48,36},{60,72},{72,60},{84,96},{96,84},{1... | collective-permute-start | bytes 580616 | tf_op jit(solution)/shard_map/ppermute | solution.py:393
  36.9 0.0 collective-permute-done.2.levels
  36.9 0.5 %shard_map.121 = f32[189,256]{1,0:T(8,128)S(1)} custom-call(s32[4,256]{1,0:T(4,128)S(1)} %get-tuple-element.29.send, s32[2,128]{1,0:T(2,128)S(1)} %collective-permute-done.2.levels, bf16[432,1536]{1,0:T(8,128)(2,1)S(1)} %get-tuple-element.36.table), custom_call_target="tpu_custom_call" | custom-call | flops 300000000 | bytes 2659328 | tf_op jit(solution)/shard_map/pallas_call | solution.py:373
  37.5 3.9 %collective-permute-start.3 = (f32[189,256]{1,0:T(8,128)S(1)}, f32[189,256]{1,0:T(8,128)S(1)}, u32[]{:S(2)}, u32[]{:S(2)}) collective-permute-start(f32[189,256]{1,0:T(8,128)S(1)} %shard_map.121), channel_id=1, source_target_pairs={{1,2},{2,1},{3,4},{4,3},{5,6},{6,5},{7,8},{8,7},{9,10},{10,9},{13,... | collective-permute-start | bytes 580616 | tf_op jit(solution)/shard_map/ppermute | solution.py:393
  41.4 2.4 %shard_map.122 = (f32[9,56,128]{2,1,0:T(8,128)S(1)}, f32[216,512]{1,0:T(8,128)S(1)}, f32[8,512]{1,0:T(8,128)S(1)}, f32[56,288]{1,0:T(8,128)S(1)}, bf16[512,1024]{1,0:T(8,128)(2,1)S(1)}) custom-call(f32[9,9,128]{2,1,0:T(8,128)S(1)} %get-tuple-element.38.flux_inner, f32[9,56,128]{2,1,0:T(8,128)S(1)} %get-tuple-element.31.state, ...), custom_call_target="tpu_custom_call" | custom-call | flops 1000000000 | bytes 3399808 | tf_op jit(solution)/shard_map/pallas_call | solution.py:373
  43.8 0.0 collective-permute-done.4.arrive_a
  43.8 0.0 collective-permute-done.5.arrive_c
  43.8 0.4 shard_map.125.outer
  44.2 0.5 %collective-permute-done.1.arrive_b = f32[189,256]{1,0:T(8,128)S(1)} collective-permute-done((f32[189,256]{1,0:T(8,128)S(1)}, f32[189,256]{1,0:T(8,128)S(1)}, u32[]{:S(2)}, u32[]{:S(2)}) %collective-permute-start.1) | collective-permute-done | bytes 193568 | tf_op jit(solution)/shard_map/ppermute | solution.py:393
  44.8 3.2 %collective-permute-done.3.arrive_d = f32[189,256]{1,0:T(8,128)S(1)} collective-permute-done((f32[189,256]{1,0:T(8,128)S(1)}, f32[189,256]{1,0:T(8,128)S(1)}, u32[]{:S(2)}, u32[]{:S(2)}) %collective-permute-start.3) | collective-permute-done | bytes 193568 | tf_op jit(solution)/shard_map/ppermute | solution.py:393
  48.0 1.4 %shard_map.126 = f32[9,56,128]{2,1,0:T(8,128)} custom-call(f32[9,9,128]{2,1,0:T(8,128)S(1)} %get-tuple-element.28.flux_outer, f32[189,256]{1,0:T(8,128)S(1)} %collective-permute-done.1.arrive_b, f32[189,256]{1,0:T(8,128)S(1)} %collective-permute-done.3.arrive_d, bf16[512,1024]{1,0:T(8,128)(2,1)S(1)} %get-tuple-element.44.arrive_hot, ...), custom_call_target="tpu_custom_call" | custom-call | flops 500000000 | bytes 3307008 | tf_op jit(solution)/shard_map/pallas_call | solution.py:373
  (1 shorter events, 0.0 us)
Async XLA Ops:
  7.1 36.7 %collective-permute-start.4 = (f32[3,189,256]{2,1,0:T(8,128)S(1)}, f32[3,189,256]{2,1,0:T(8,128)S(1)}, u32[]{:S(2)}, u32[]{:S(2)}) collective-permute-start(f32[3,189,256]{2,1,0:T(8,128)S(1)} %shard_map.123), channel_id=1, source_target_pairs={{0,12},{12,0},{24,36},{36,24},{48,60},{60,48},{72,84},{84,72},{96,... | collective-permute-start | bytes 1741832 | tf_op jit(solution)/shard_map/ppermute | solution.py:393
  9.5 34.3 %collective-permute-start.5 = (f32[3,189,256]{2,1,0:T(8,128)S(1)}, f32[3,189,256]{2,1,0:T(8,128)S(1)}, u32[]{:S(2)}, u32[]{:S(2)}) collective-permute-start(f32[3,189,256]{2,1,0:T(8,128)S(1)} %shard_map.124), channel_id=1, source_target_pairs={{0,1},{1,0},{2,3},{3,2},{4,5},{5,4},{6,7},{7,6},{8,9},{9,8},{10,11... | collective-permute-start | bytes 1741832 | tf_op jit(solution)/shard_map/ppermute | solution.py:393
  12.9 17.4 %collective-permute-start = (s32[2,128]{1,0:T(2,128)S(1)}, s32[2,128]{1,0:T(2,128)S(1)}, u32[]{:S(2)}, u32[]{:S(2)}) collective-permute-start(s32[2,128]{1,0:T(2,128)S(1)} %get-tuple-element.30), channel_id=1, source_target_pairs={{12,24},{24,12},{36,48},{48,36},{60,72},{72,60},{84,96},{96,84},{1... | collective-permute-start | bytes 3080 | tf_op jit(solution)/shard_map/ppermute | solution.py:393
  26.3 10.6 %collective-permute-start.2 = (s32[2,128]{1,0:T(2,128)S(1)}, s32[2,128]{1,0:T(2,128)S(1)}, u32[]{:S(2)}, u32[]{:S(2)}) collective-permute-start(s32[2,128]{1,0:T(2,128)S(1)} %get-tuple-element.37), channel_id=1, source_target_pairs={{1,2},{2,1},{3,4},{4,3},{5,6},{6,5},{7,8},{8,7},{9,10},{10,9},{13,... | collective-permute-start | bytes 3080 | tf_op jit(solution)/shard_map/ppermute | solution.py:393
  30.8 13.9 %collective-permute-start.1 = (f32[189,256]{1,0:T(8,128)S(1)}, f32[189,256]{1,0:T(8,128)S(1)}, u32[]{:S(2)}, u32[]{:S(2)}) collective-permute-start(f32[189,256]{1,0:T(8,128)S(1)} %shard_map.120), channel_id=1, source_target_pairs={{12,24},{24,12},{36,48},{48,36},{60,72},{72,60},{84,96},{96,84},{1... | collective-permute-start | bytes 580616 | tf_op jit(solution)/shard_map/ppermute | solution.py:393
  37.5 10.5 %collective-permute-start.3 = (f32[189,256]{1,0:T(8,128)S(1)}, f32[189,256]{1,0:T(8,128)S(1)}, u32[]{:S(2)}, u32[]{:S(2)}) collective-permute-start(f32[189,256]{1,0:T(8,128)S(1)} %shard_map.121), channel_id=1, source_target_pairs={{1,2},{2,1},{3,4},{4,3},{5,6},{6,5},{7,8},{8,7},{9,10},{10,9},{13,... | collective-permute-start | bytes 580616 | tf_op jit(solution)/shard_map/ppermute | solution.py:393

commit v2 on v1

--- a/solution.py
+++ b/solution.py
@@ -73,18 +73,24 @@
     return jnp.concatenate([ref[0:1, :], ref[1:2, :]], axis=1)
 
 
-def fill_modal(modal, left, pieces):
-    for first in range(0, FIELDS * COUNT, 2 * COUNT):
-        columns = slice(first, min(first + 2 * COUNT, FIELDS * COUNT))
-        right = jnp.concatenate([pieces[:, columns], pieces[0:64, columns]], axis=0)
-        modal[:, columns] = matmul(left[...], right)
+def fill_modal(modal, left, pieces, first):
+    right = jnp.concatenate([pieces[first + at] for at in range(3)], axis=1)
+    both = matmul(left[...], jnp.concatenate([right, right[0:64]], axis=0))
+    for at in range(3):
+        modal[first + at] = both[:, at * COUNT : (at + 1) * COUNT]
+
+
+def place_pieces(pieces, at, value):
+    high, low = split(value)
+    pieces[at, 0:MODES, :] = high
+    pieces[at, 64 : 64 + MODES, :] = low
 
 
 def mix_star(modal, star, group):
     sums = [None] * len(group)
     for d in range(3):
         for q in range(FIELDS):
-            value = modal[d * MODES : (d + 1) * MODES, q * COUNT : (q + 1) * COUNT]
+            value = modal[q, d * MODES : (d + 1) * MODES, :]
             for at, p in enumerate(group):
                 term = star[q, p, d : d + 1, :] * value
                 sums[at] = term if sums[at] is None else sums[at] + term
@@ -146,7 +152,7 @@
 def taylor_kernel(
     state, star, stiffness, face_project, level,
     table, own,
-    wide, left, face_left, stack, modal, pieces, level_pieces,
+    wide, left, face_left, stack, modal_even, modal_odd, pieces, level_pieces,
 ):
     wide[...] = jnp.zeros_like(wide)
     for d in range(3):
@@ -162,19 +168,16 @@
     for q in range(FIELDS):
         value = state[q]
         stack[0, q] = value
-        high, low = split(value)
-        pieces[0:MODES, q * COUNT : (q + 1) * COUNT] = high
-        pieces[64 : 64 + MODES, q * COUNT : (q + 1) * COUNT] = low
+        place_pieces(pieces, q, value)
 
     def step(degree, carry):
-        fill_modal(modal, left, pieces)
+        for first in range(0, FIELDS, 3):
+            fill_modal(modal_even, left, pieces, first)
         for first in range(0, FIELDS, 3):
             group = range(first, first + 3)
-            for p, value in zip(group, mix_star(modal, star, group)):
+            for p, value in zip(group, mix_star(modal_even, star, group)):
                 stack[degree + 1, p] = value
-                high, low = split(value)
-                pieces[0:MODES, p * COUNT : (p + 1) * COUNT] = high
-                pieces[64 : 64 + MODES, p * COUNT : (p + 1) * COUNT] = low
+                place_pieces(pieces, p, value)
         return carry
 
     lax.fori_loop(0, ORDER - 1, step, 0)
@@ -205,6 +208,27 @@
                 table[q * 48 : q * 48 + 48, column : column + COUNT] = jnp.concatenate(
                     [high, low], axis=0
                 ).astype(bf16)
+
+
+def starts_early():
+    return lax.rem(lax.axis_index("gx"), 8) == 0
+
+
+def taylor_early_kernel(*refs):
+    @pl.when(starts_early())
+    def _():
+        taylor_kernel(*refs)
+
+
+def taylor_late_kernel(*refs):
+    @pl.when(jnp.logical_not(starts_early()))
+    def _():
+        taylor_kernel(*refs[:5], *refs[7:])
+
+    @pl.when(starts_early())
+    def _():
+        refs[7][...] = refs[5][...]
+        refs[8][...] = refs[6][...]
 
 
 def put(out, found):
@@ -265,15 +289,14 @@
     left[...] = wide[0:224, 0:192].astype(bf16)
     pieces[...] = jnp.zeros_like(pieces)
     for q in range(FIELDS):
-        high, low = split(own[q])
-        pieces[0:MODES, q * COUNT : (q + 1) * COUNT] = high
-        pieces[64 : 64 + MODES, q * COUNT : (q + 1) * COUNT] = low
-    fill_modal(modal, left, pieces)
+        place_pieces(pieces, q, own[q])
+    for first in range(0, FIELDS, 3):
+        fill_modal(modal, left, pieces, first)
     for first in range(0, FIELDS, 3):
         group = range(first, first + 3)
         sums = mix_star(modal, star, group)
         for q in range(FIELDS):
-            value = modal[168:224, q * COUNT : (q + 1) * COUNT]
+            value = modal[q, 168:224, :]
             for at, p in enumerate(group):
                 sums[at] = sums[at] + flux_inner[q, p : p + 1, :] * value
         for at, p in enumerate(group):
@@ -319,11 +342,12 @@
     return jnp.where(levels == 0, arrive[0, rows, :], jnp.where(levels == 1, arrive[1, rows, :], arrive[2, rows, :]))
 
 
-def absorb_kernel(level_a, level_c, arrive_a, arrive_c, arrive_hot, outer, total, arrived):
+def absorb_kernel(level_a, level_c, arrive_a, arrive_c, arrive_b, arrive_hot, outer, total, arrived):
     for at, (level, arrive) in enumerate(((level_a, arrive_a), (level_c, arrive_c))):
         levels = pair_row(level)
         place_arrived(arrived, at, lambda rows: picked(levels, arrive, rows))
-    found = matmul_nt(arrived[...], arrive_hot[:, 0:512])
+    place_arrived(arrived, 2, lambda rows: arrive_b[rows, :])
+    found = matmul_nt(arrived[...], arrive_hot[:, 0:768])
     for q in range(FIELDS):
         total[q * 24 : q * 24 + 24, :] = (
             outer[q * 24 : q * 24 + 24, :] + found[q * 48 : q * 48 + 24, :] + found[q * 48 + 24 : q * 48 + 48, :]
@@ -331,13 +355,12 @@
 
 
 def final_kernel(
-    flux_outer, arrive_b, arrive_d, arrive_hot, base, outer, keep, lift_left,
+    flux_outer, arrive_d, arrive_hot, base, outer, keep, lift_left,
     updated,
     arrived, lifted_right, lifted,
 ):
-    place_arrived(arrived, 0, lambda rows: arrive_b[rows, :])
-    place_arrived(arrived, 1, lambda rows: arrive_d[rows, :])
-    found = matmul_nt(arrived[...], arrive_hot[:, 512:1024])
+    place_arrived(arrived, 0, lambda rows: arrive_d[rows, :])
+    found = matmul_nt(arrived[...], arrive_hot[:, 768:1024])
     for q in range(FIELDS):
         total = found[q * 48 : q * 48 + 24, :] + found[q * 48 + 24 : q * 48 + 48, :] + outer[q * 24 : q * 24 + 24, :]
         if 3 <= q < 6:
@@ -422,25 +445,23 @@
         (odd,), inputs, 1000, pltpu.HBM,
     )
     flux_inner, flux_outer, state, star, level_a, level_c, want_b, want_d = rest
+    taylor_outs = (shape(FIELDS * 48, LEVELS * 4 * COUNT, dtype=bf16), shape(FIELDS, MODES, COUNT))
+    taylor_scratch = [
+        pltpu.VMEM((224, 256), f32),
+        pltpu.VMEM((168, 192), bf16),
+        pltpu.VMEM((96, 192), bf16),
+        pltpu.VMEM((ORDER, FIELDS, MODES, COUNT), f32),
+        pltpu.VMEM((FIELDS, 168, COUNT), f32),
+        pltpu.VMEM((FIELDS, 168, COUNT), f32),
+        pltpu.VMEM((FIELDS, 128, COUNT), bf16),
+        pltpu.VMEM((128, LEVELS * FIELDS * COUNT), bf16),
+    ]
+    taylor_inputs = (state, star, stiffness, face_project, level)
+    early = call(taylor_early_kernel, taylor_outs, taylor_scratch, (), taylor_inputs, 2000000000)
     level_b = swapped(want_b, "gx", 1)
     level_d = swapped(want_d, "gy", 1)
 
-    table, own = call(
-        taylor_kernel,
-        (shape(FIELDS * 48, LEVELS * 4 * COUNT, dtype=bf16), shape(FIELDS, MODES, COUNT)),
-        [
-            pltpu.VMEM((224, 256), f32),
-            pltpu.VMEM((168, 192), bf16),
-            pltpu.VMEM((96, 192), bf16),
-            pltpu.VMEM((ORDER, FIELDS, MODES, COUNT), f32),
-            pltpu.VMEM((168, FIELDS * COUNT), f32),
-            pltpu.VMEM((128, FIELDS * COUNT), bf16),
-            pltpu.VMEM((128, LEVELS * FIELDS * COUNT), bf16),
-        ],
-        (),
-        (state, star, stiffness, face_project, level),
-        2000000000,
-    )
+    table, own = call(taylor_late_kernel, taylor_outs, taylor_scratch, (), taylor_inputs + tuple(early), 2000000000)
     piece, pieces = shape(ROWS, SLOTS), shape(LEVELS, ROWS, SLOTS)
 
     def gathered(at, levels):
@@ -470,25 +491,24 @@
             pltpu.VMEM((128, 128), f32),
             pltpu.VMEM((224, 256), f32),
             pltpu.VMEM((224, 192), bf16),
-            pltpu.VMEM((128, FIELDS * COUNT), bf16),
-            pltpu.VMEM((224, FIELDS * COUNT), f32),
+            pltpu.VMEM((FIELDS, 128, COUNT), bf16),
+            pltpu.VMEM((FIELDS, 224, COUNT), f32),
             pltpu.VMEM((LEVELS * 4 * COUNT, 4 * COUNT), bf16),
         ],
         (),
         (flux_inner, state, star, stiffness, face_project, level, neighbour, fault, flags, receive, table, own),
         1000000000,
     )
-    arrived = pltpu.VMEM((FIELDS * 48, 2 * SLOTS), bf16)
     outer = call(
-        absorb_kernel, shape(FIELDS * 24, 4 * COUNT), [arrived], (),
-        (level_a, level_c, arrive_a, arrive_c, arrive_hot, outer), 300000000,
+        absorb_kernel, shape(FIELDS * 24, 4 * COUNT), [pltpu.VMEM((FIELDS * 48, 3 * SLOTS), bf16)], (),
+        (level_a, level_c, arrive_a, arrive_c, arrive_b, arrive_hot, outer), 300000000,
     )
     return call(
         final_kernel,
         shape(FIELDS, MODES, COUNT),
-        [arrived, pltpu.VMEM((288, FIELDS * COUNT), bf16), pltpu.VMEM((MODES, FIELDS * COUNT), f32)],
+        [pltpu.VMEM((FIELDS * 48, SLOTS), bf16), pltpu.VMEM((288, FIELDS * COUNT), bf16), pltpu.VMEM((MODES, FIELDS * COUNT), f32)],
         (),
-        (flux_outer, arrive_b, arrive_d, arrive_hot, base, outer, keep, lift_left),
+        (flux_outer, arrive_d, arrive_hot, base, outer, keep, lift_left),
         500000000,
     )
 

time: 49.7 us -> 49.6 us (level)
  the two profiles are of different devices: /device:TPU:96 before, /device:TPU:112 now
where the time goes in v2:
time: 49.6 us; the launch traced here: 49.3 us
  starting transfers between devices  32.3 us (65%)
  Pallas kernels  12.8 us (26%)
  waiting for transfers between devices  4 us (8%)
    ppermute x6, starting transfers between devices, swapped(): return lax.ppermute(value, axis, pairs)  32.3 us
    pallas_call x10, Pallas kernels, call(): pl.pallas_call(kernel, out_shape=outs, in_specs=[spec()] * len(near) + [s...  12.8 us
    ppermute x6, waiting for transfers between devices, swapped(): return lax.ppermute(value, axis, pairs)  4 us
  transfers between devices with their start and end apart: 6, of which 2 were waited for; matrix products, arithmetic and copies ran while one was open for 0% of the time, Pallas kernels for 9%

profile of v2, /device:TPU:112, one launch (start us, length us, event | category | flops | bytes accessed | tf_op | source)
XLA Modules:
  0.0 49.3 jit_solution(11700708433003379272)
XLA Ops:
  0.0 0.1 iota.7.odd
  0.1 1.3 %shard_map.118 = (s32[1,128]{1,0:T(1,128)S(1)}, s32[4,256]{1,0:T(4,128)S(1)}, s32[4,256]{1,0:T(4,128)S(1)}, f32[3,56,56]{2,1,0:T(8,128)S(1)}, f32[4,21,56]{2,1,0...) custom-call(s32[8,256]{1,0:T(8,128)S(1)} %iota.7.odd, ...), custom_call_target="tpu_custom_call" | custom-call | flops 1000 | bytes 450824 | tf_op jit(solution)/shard_map/pallas_call | solution.py:396
  1.4 5.1 %shard_map.119 = (bf16[432,1536]{1,0:T(8,128)(2,1)S(1)}, f32[9,56,128]{2,1,0:T(8,128)S(1)}) custom-call(f32[9,56,128]{2,1,0:T(8,128)S(1)} %get-tuple-element.33.refs_0_.state, f32[9,9,3,128]{3,2,1,0:T(4,128)S(1)} %get-tuple-element.34.refs_1_.star, f32[3,56,56]{2,1,0:T(8,128)S(1)} %get-tuple-element.35.refs_2_.stiffness, ...), custom_call_target="tpu_custom_call" | custom-call | flops 2000000000 | bytes 439424 | tf_op jit(solution)/shard_map/pallas_call | solution.py:396
  6.5 0.1 shard_map.120
  6.7 0.5 %shard_map.123 = f32[3,189,256]{2,1,0:T(8,128)S(1)} custom-call(s32[4,256]{1,0:T(4,128)S(1)} %get-tuple-element.31.send, bf16[432,1536]{1,0:T(8,128)(2,1)S(1)} %get-tuple-element.40.table), custom_call_target="tpu_custom_call" | custom-call | flops 300000000 | bytes 2658304 | tf_op jit(solution)/shard_map/pallas_call | solution.py:396
  7.2 1.9 %collective-permute-start.2 = (f32[3,189,256]{2,1,0:T(8,128)S(1)}, f32[3,189,256]{2,1,0:T(8,128)S(1)}, u32[]{:S(2)}, u32[]{:S(2)}) collective-permute-start(f32[3,189,256]{2,1,0:T(8,128)S(1)} %shard_map.123), channel_id=1, source_target_pairs={{0,12},{12,0},{24,36},{36,24},{48,60},{60,48},{72,84},{84,72},{96,... | collective-permute-start | bytes 1741832 | tf_op jit(solution)/shard_map/ppermute | solution.py:416
  9.1 0.5 %shard_map.124 = f32[3,189,256]{2,1,0:T(8,128)S(1)} custom-call(s32[4,256]{1,0:T(4,128)S(1)} %get-tuple-element.31.send, bf16[432,1536]{1,0:T(8,128)(2,1)S(1)} %get-tuple-element.40.table), custom_call_target="tpu_custom_call" | custom-call | flops 300000000 | bytes 2658304 | tf_op jit(solution)/shard_map/pallas_call | solution.py:396
  9.6 3.4 %collective-permute-start.3 = (f32[3,189,256]{2,1,0:T(8,128)S(1)}, f32[3,189,256]{2,1,0:T(8,128)S(1)}, u32[]{:S(2)}, u32[]{:S(2)}) collective-permute-start(f32[3,189,256]{2,1,0:T(8,128)S(1)} %shard_map.124), channel_id=1, source_target_pairs={{0,1},{1,0},{2,3},{3,2},{4,5},{5,4},{6,7},{7,6},{8,9},{9,8},{10,11... | collective-permute-start | bytes 1741832 | tf_op jit(solution)/shard_map/ppermute | solution.py:416
  13.1 14.2 %collective-permute-start.4 = (s32[2,128]{1,0:T(2,128)S(1)}, s32[2,128]{1,0:T(2,128)S(1)}, u32[]{:S(2)}, u32[]{:S(2)}) collective-permute-start(s32[2,128]{1,0:T(2,128)S(1)} %get-tuple-element.51), channel_id=1, source_target_pairs={{12,24},{24,12},{36,48},{48,36},{60,72},{72,60},{84,96},{96,84},{1... | collective-permute-start | bytes 3080 | tf_op jit(solution)/shard_map/ppermute | solution.py:416
  27.2 4.0 %collective-permute-start = (s32[2,128]{1,0:T(2,128)S(1)}, s32[2,128]{1,0:T(2,128)S(1)}, u32[]{:S(2)}, u32[]{:S(2)}) collective-permute-start(s32[2,128]{1,0:T(2,128)S(1)} %get-tuple-element.32), channel_id=1, source_target_pairs={{1,2},{2,1},{3,4},{4,3},{5,6},{6,5},{7,8},{8,7},{9,10},{10,9},{13,... | collective-permute-start | bytes 3080 | tf_op jit(solution)/shard_map/ppermute | solution.py:416
  31.2 0.0 collective-permute-done.4.levels
  31.2 0.5 %shard_map.125 = f32[189,256]{1,0:T(8,128)S(1)} custom-call(s32[4,256]{1,0:T(4,128)S(1)} %get-tuple-element.31.send, s32[2,128]{1,0:T(2,128)S(1)} %collective-permute-done.4.levels, bf16[432,1536]{1,0:T(8,128)(2,1)S(1)} %get-tuple-element.40.table), custom_call_target="tpu_custom_call" | custom-call | flops 300000000 | bytes 2659328 | tf_op jit(solution)/shard_map/pallas_call | solution.py:396
  31.8 4.9 %collective-permute-start.5 = (f32[189,256]{1,0:T(8,128)S(1)}, f32[189,256]{1,0:T(8,128)S(1)}, u32[]{:S(2)}, u32[]{:S(2)}) collective-permute-start(f32[189,256]{1,0:T(8,128)S(1)} %shard_map.125), channel_id=1, source_target_pairs={{12,24},{24,12},{36,48},{48,36},{60,72},{72,60},{84,96},{96,84},{1... | collective-permute-start | bytes 580616 | tf_op jit(solution)/shard_map/ppermute | solution.py:416
  36.7 0.0 collective-permute-done.levels
  36.7 0.5 %shard_map.121 = f32[189,256]{1,0:T(8,128)S(1)} custom-call(s32[4,256]{1,0:T(4,128)S(1)} %get-tuple-element.31.send, s32[2,128]{1,0:T(2,128)S(1)} %collective-permute-done.levels, bf16[432,1536]{1,0:T(8,128)(2,1)S(1)} %get-tuple-element.40.table), custom_call_target="tpu_custom_call" | custom-call | flops 300000000 | bytes 2659328 | tf_op jit(solution)/shard_map/pallas_call | solution.py:396
  37.2 3.9 %collective-permute-start.1 = (f32[189,256]{1,0:T(8,128)S(1)}, f32[189,256]{1,0:T(8,128)S(1)}, u32[]{:S(2)}, u32[]{:S(2)}) collective-permute-start(f32[189,256]{1,0:T(8,128)S(1)} %shard_map.121), channel_id=1, source_target_pairs={{1,2},{2,1},{3,4},{4,3},{5,6},{6,5},{7,8},{8,7},{9,10},{10,9},{13,... | collective-permute-start | bytes 580616 | tf_op jit(solution)/shard_map/ppermute | solution.py:416
  41.1 2.4 %shard_map.122 = (f32[9,56,128]{2,1,0:T(8,128)S(1)}, f32[216,512]{1,0:T(8,128)S(1)}, f32[8,512]{1,0:T(8,128)S(1)}, f32[56,288]{1,0:T(8,128)S(1)}, bf16[512,1024]{1,0:T(8,128)(2,1)S(1)}) custom-call(f32[9,9,128]{2,1,0:T(8,128)S(1)} %get-tuple-element.41.flux_inner, f32[9,56,128]{2,1,0:T(8,128)S(1)} %get-tuple-element.33.refs_0_.state, ...), custom_call_target="tpu_custom_call" | custom-call | flops 1000000000 | bytes 3399808 | tf_op jit(solution)/shard_map/pallas_call | solution.py:396
  43.5 0.7 %collective-permute-done.5.arrive_b = f32[189,256]{1,0:T(8,128)S(1)} collective-permute-done((f32[189,256]{1,0:T(8,128)S(1)}, f32[189,256]{1,0:T(8,128)S(1)}, u32[]{:S(2)}, u32[]{:S(2)}) %collective-permute-start.5) | collective-permute-done | bytes 193568 | tf_op jit(solution)/shard_map/ppermute | solution.py:416
  44.1 0.0 collective-permute-done.2.arrive_a
  44.1 0.0 collective-permute-done.3.arrive_c
  44.1 0.6 %shard_map.126.outer = f32[216,512]{1,0:T(8,128)S(1)} custom-call(s32[2,128]{1,0:T(2,128)S(1)} %get-tuple-element.49.level_a, s32[2,128]{1,0:T(2,128)S(1)} %get-tuple-element.50.level_c, f32[3,189,256]{2,1,0:T(8,128)S(1)} %collective-permute-done.2.arrive_a, f32[3,189,256]{2,1,0:T(8,128)S(1)} %collective-permute-done.3.arrive_c, ...), custom_call_target="tpu_custom_call" | custom-call | flops 300000000 | bytes 3896320 | tf_op jit(solution)/shard_map/pallas_call | solution.py:396
  44.7 3.3 %collective-permute-done.1.arrive_d = f32[189,256]{1,0:T(8,128)S(1)} collective-permute-done((f32[189,256]{1,0:T(8,128)S(1)}, f32[189,256]{1,0:T(8,128)S(1)}, u32[]{:S(2)}, u32[]{:S(2)}) %collective-permute-start.1) | collective-permute-done | bytes 193568 | tf_op jit(solution)/shard_map/ppermute | solution.py:416
  48.0 1.3 %shard_map.127 = f32[9,56,128]{2,1,0:T(8,128)} custom-call(f32[9,9,128]{2,1,0:T(8,128)S(1)} %get-tuple-element.30.flux_outer, f32[189,256]{1,0:T(8,128)S(1)} %collective-permute-done.1.arrive_d, bf16[512,1024]{1,0:T(8,128)(2,1)S(1)} %get-tuple-element.47.arrive_hot, f32[9,56,128]{2,1,0:T(8,128)S(1)} %get-tuple-element.48.base, ...), custom_call_target="tpu_custom_call" | custom-call | flops 500000000 | bytes 3113472 | tf_op jit(solution)/shard_map/pallas_call | solution.py:396
  (1 shorter events, 0.0 us)
Async XLA Ops:
  7.2 37.0 %collective-permute-start.2 = (f32[3,189,256]{2,1,0:T(8,128)S(1)}, f32[3,189,256]{2,1,0:T(8,128)S(1)}, u32[]{:S(2)}, u32[]{:S(2)}) collective-permute-start(f32[3,189,256]{2,1,0:T(8,128)S(1)} %shard_map.123), channel_id=1, source_target_pairs={{0,12},{12,0},{24,36},{36,24},{48,60},{60,48},{72,84},{84,72},{96,... | collective-permute-start | bytes 1741832 | tf_op jit(solution)/shard_map/ppermute | solution.py:416
  9.6 34.5 %collective-permute-start.3 = (f32[3,189,256]{2,1,0:T(8,128)S(1)}, f32[3,189,256]{2,1,0:T(8,128)S(1)}, u32[]{:S(2)}, u32[]{:S(2)}) collective-permute-start(f32[3,189,256]{2,1,0:T(8,128)S(1)} %shard_map.124), channel_id=1, source_target_pairs={{0,1},{1,0},{2,3},{3,2},{4,5},{5,4},{6,7},{7,6},{8,9},{9,8},{10,11... | collective-permute-start | bytes 1741832 | tf_op jit(solution)/shard_map/ppermute | solution.py:416
  13.1 18.2 %collective-permute-start.4 = (s32[2,128]{1,0:T(2,128)S(1)}, s32[2,128]{1,0:T(2,128)S(1)}, u32[]{:S(2)}, u32[]{:S(2)}) collective-permute-start(s32[2,128]{1,0:T(2,128)S(1)} %get-tuple-element.51), channel_id=1, source_target_pairs={{12,24},{24,12},{36,48},{48,36},{60,72},{72,60},{84,96},{96,84},{1... | collective-permute-start | bytes 3080 | tf_op jit(solution)/shard_map/ppermute | solution.py:416
  27.2 9.4 %collective-permute-start = (s32[2,128]{1,0:T(2,128)S(1)}, s32[2,128]{1,0:T(2,128)S(1)}, u32[]{:S(2)}, u32[]{:S(2)}) collective-permute-start(s32[2,128]{1,0:T(2,128)S(1)} %get-tuple-element.32), channel_id=1, source_target_pairs={{1,2},{2,1},{3,4},{4,3},{5,6},{6,5},{7,8},{8,7},{9,10},{10,9},{13,... | collective-permute-start | bytes 3080 | tf_op jit(solution)/shard_map/ppermute | solution.py:416
  31.8 12.4 %collective-permute-start.5 = (f32[189,256]{1,0:T(8,128)S(1)}, f32[189,256]{1,0:T(8,128)S(1)}, u32[]{:S(2)}, u32[]{:S(2)}) collective-permute-start(f32[189,256]{1,0:T(8,128)S(1)} %shard_map.125), channel_id=1, source_target_pairs={{12,24},{24,12},{36,48},{48,36},{60,72},{72,60},{84,96},{96,84},{1... | collective-permute-start | bytes 580616 | tf_op jit(solution)/shard_map/ppermute | solution.py:416
  37.2 10.8 %collective-permute-start.1 = (f32[189,256]{1,0:T(8,128)S(1)}, f32[189,256]{1,0:T(8,128)S(1)}, u32[]{:S(2)}, u32[]{:S(2)}) collective-permute-start(f32[189,256]{1,0:T(8,128)S(1)} %shard_map.121), channel_id=1, source_target_pairs={{1,2},{2,1},{3,4},{4,3},{5,6},{6,5},{7,8},{8,7},{9,10},{10,9},{13,... | collective-permute-start | bytes 580616 | tf_op jit(solution)/shard_map/ppermute | solution.py:416
